TPU v7x, 512 devices: a whole 4x8x8 slice. The times are simulated.
512 devices in a mesh: sample: 4 (over y_lo), variant: 32 (over x, z), trait: 4 (over y_hi, core).
Axes of the slice: x: 4, y: 8 (y_hi: 2, y_lo: 4; y = y_hi * 4 + y_lo), z: 8, core: 2. Of those that a mesh axis runs over, the one named last changes fastest.
Arguments:
- dosages: bfloat16 [4096, 65536], P('sample', 'variant')
- phenotypes: float32 [4096, 64], P('sample', 'trait')
- batch_rows: int32 [8, 4096], P(None, 'sample'), may hold values from 0 to 1023
Outputs:
- weights: float32 [64, 65536], P('trait', 'variant')
Inputs may be any that keep to these rules, and one draw needn't show every extreme that they name: Draw j of iteration t refers to sample (j // 1024) * 1024 + batch_rows[t-1, j]; draws repeat.
All inputs are finite; a program needn't handle non-finite values.
Results may differ from a plain program's by a relative error of at most 0.0025.
Values may be sent and summed in bfloat16 or wider, within the bound.
A program may use at most 64 MiB of HBM per device.

v0:
```python
import math

import jax
import jax.numpy as jnp
from jax import lax
from jax.sharding import PartitionSpec as P

ITERS = 8


def trait_power(dual):
    squares = jnp.sum(dual * dual, axis=0)
    return lax.psum(squares, "trait")


def on_device(dosages, phenotypes, batch_rows):
    local_rows = dosages.shape[0]
    group_size = lax.axis_size("sample")
    total_variants = dosages.shape[1] * lax.axis_size("variant")
    total_draws = batch_rows.shape[1] * group_size
    pred_scale = 0.06 * math.sqrt(total_draws) / total_variants
    grad_scale = 1.0 / math.sqrt(total_draws)
    width_traits = phenotypes.shape[1]
    width_cols = dosages.shape[1]
    dual = jnp.zeros((width_traits, width_cols), jnp.float32)
    weights_full = jnp.zeros((width_traits, width_cols), jnp.float32)
    weights_low = weights_full.astype(jnp.bfloat16)
    for step in range(ITERS):
        turn = step + 1
        counts = jnp.zeros((local_rows,), jnp.float32).at[batch_rows[step]].add(1.0)
        if step == 0:
            predictions = jnp.zeros_like(phenotypes)
        else:
            partial_sum = lax.dot_general(
                dosages, weights_low, (((1,), (1,)), ((), ())), preferred_element_type=jnp.float32
            )
            predictions = (
                lax.psum(partial_sum.astype(jnp.bfloat16), "variant").astype(jnp.float32)
                * pred_scale
            )
        misfit = (counts[:, None] * (predictions - phenotypes)).astype(jnp.bfloat16)
        grad_part = lax.dot_general(
            misfit, dosages, (((0,), (0,)), ((), ())), preferred_element_type=jnp.float32
        )
        gradient = lax.psum(grad_part, "sample") * grad_scale
        dual = dual + (gradient - dual) / turn
        power = trait_power(dual)
        shrink = jax.nn.relu(1.0 - 20.0 / jnp.sqrt(power + 1e-05))
        weights_full = -math.sqrt(turn) * shrink[None, :] * dual
        weights_low = weights_full.astype(jnp.bfloat16)
    return weights_full


def solution(mesh):
    return jax.shard_map(
        on_device,
        mesh=mesh,
        in_specs=(P("sample", "variant"), P("sample", "trait"), P(None, "sample")),
        out_specs=P("trait", "variant"),
        check_vma=False,
    )
```

profile of v0, /device:TPU:1, one launch (start us, length us, event | category | flops | bytes accessed | tf_op | source)
XLA Modules:
  0.0 1546.0 jit_solution(12416131265628424412)
XLA Ops:
  6.5 1.1 compare_select_fusion
  7.6 7.6 scatter_custom_fusion
  15.3 3.6 fusion.14
  18.9 0.0 all-reduce.11.cloned.1.call-start
  18.9 7.6 scatter_custom_fusion.1
  26.6 49.9 %all-reduce.9.cloned.1.call-done = f32[16,2048]{1,0:T(8,128)} async-done(((f32[16,2048]{1,0:T(8,128)}), f32[16,2048]{1,0:T(8,128)}) %all-reduce.9.cloned.1.call-update) | async-done | bytes 131088 | tf_op jit(solution)/shard_map/psum | solution.py:45
  76.5 0.9 multiply_reduce_fusion.7
  77.4 11.7 psum.162
  89.2 3.5 fusion
  92.7 116.2 %psum.163 = bf16[1024,16]{0,1:T(8,128)(2,1)S(1)} all-reduce(bf16[1024,16]{0,1:T(8,128)(2,1)S(1)} %fusion), channel_id=1, replica_groups=mesh['sample'=4,'variant'=32,'trait'=4] {'variant'}, use_global_device_ids=true, to_apply=%region_5.6 | all-reduce | flops 16384 | bytes 65536 | tf_op jit(solution)/shard_map/psum | solution.py:38
  208.9 3.5 fusion.15
  212.4 0.0 all-reduce.11.cloned.1.call-update
  212.4 0.0 all-reduce.13.cloned.1.call-start
  212.4 7.6 scatter_custom_fusion.2
  220.1 63.4 %all-reduce.11.cloned.1.call-done = f32[16,2048]{1,0:T(8,128)} async-done(((f32[16,2048]{1,0:T(8,128)}), f32[16,2048]{1,0:T(8,128)}) %all-reduce.11.cloned.1.call-update) | async-done | bytes 131088 | tf_op jit(solution)/shard_map/psum | solution.py:45
  283.5 1.0 multiply_reduce_fusion.6
  284.4 11.7 psum.165
  296.2 3.4 fusion.1
  299.5 116.2 %psum.166 = bf16[1024,16]{0,1:T(8,128)(2,1)S(1)} all-reduce(bf16[1024,16]{0,1:T(8,128)(2,1)S(1)} %fusion.1), channel_id=1, replica_groups=mesh['sample'=4,'variant'=32,'trait'=4] {'variant'}, use_global_device_ids=true, to_apply=%region_10.11 | all-reduce | flops 16384 | bytes 65536 | tf_op jit(solution)/shard_map/psum | solution.py:38
  415.7 3.5 fusion.16
  419.2 0.0 all-reduce.15.cloned.1.call-start
  419.3 7.6 scatter_custom_fusion.3
  426.9 63.4 %all-reduce.13.cloned.1.call-done = f32[16,2048]{1,0:T(8,128)} async-done(((f32[16,2048]{1,0:T(8,128)}), f32[16,2048]{1,0:T(8,128)}) %all-reduce.13.cloned.1.call-update) | async-done | bytes 131088 | tf_op jit(solution)/shard_map/psum | solution.py:45
  490.3 0.9 multiply_reduce_fusion.5
  491.3 11.7 psum.168
  503.0 3.5 fusion.2
  506.5 116.2 %psum.169 = bf16[1024,16]{0,1:T(8,128)(2,1)S(1)} all-reduce(bf16[1024,16]{0,1:T(8,128)(2,1)S(1)} %fusion.2), channel_id=1, replica_groups=mesh['sample'=4,'variant'=32,'trait'=4] {'variant'}, use_global_device_ids=true, to_apply=%region_15.16 | all-reduce | flops 16384 | bytes 65536 | tf_op jit(solution)/shard_map/psum | solution.py:38
  622.7 3.5 fusion.17
  626.2 0.2 all-reduce.17.cloned.1.call-start
  626.4 7.6 scatter_custom_fusion.4
  634.1 63.2 %all-reduce.15.cloned.1.call-done = f32[16,2048]{1,0:T(8,128)} async-done(((f32[16,2048]{1,0:T(8,128)}), f32[16,2048]{1,0:T(8,128)}) %all-reduce.15.cloned.1.call-update) | async-done | bytes 131088 | tf_op jit(solution)/shard_map/psum | solution.py:45
  697.3 1.0 multiply_reduce_fusion.4
  698.3 11.7 psum.171
  710.0 3.4 fusion.3
  713.4 116.2 %psum.172 = bf16[1024,16]{0,1:T(8,128)(2,1)S(1)} all-reduce(bf16[1024,16]{0,1:T(8,128)(2,1)S(1)} %fusion.3), channel_id=1, replica_groups=mesh['sample'=4,'variant'=32,'trait'=4] {'variant'}, use_global_device_ids=true, to_apply=%region_20.21 | all-reduce | flops 16384 | bytes 65536 | tf_op jit(solution)/shard_map/psum | solution.py:38
  829.6 3.5 fusion.18
  833.1 0.0 all-reduce.19.cloned.1.call-start
  833.1 7.6 scatter_custom_fusion.5
  840.8 63.4 %all-reduce.17.cloned.1.call-done = f32[16,2048]{1,0:T(8,128)} async-done(((f32[16,2048]{1,0:T(8,128)}), f32[16,2048]{1,0:T(8,128)}) %all-reduce.17.cloned.1.call-update) | async-done | bytes 131088 | tf_op jit(solution)/shard_map/psum | solution.py:45
  904.2 0.9 multiply_reduce_fusion.3
  905.1 11.7 psum.174
  916.9 3.5 fusion.4
  920.4 116.2 %psum.175 = bf16[1024,16]{0,1:T(8,128)(2,1)S(1)} all-reduce(bf16[1024,16]{0,1:T(8,128)(2,1)S(1)} %fusion.4), channel_id=1, replica_groups=mesh['sample'=4,'variant'=32,'trait'=4] {'variant'}, use_global_device_ids=true, to_apply=%region_25.26 | all-reduce | flops 16384 | bytes 65536 | tf_op jit(solution)/shard_map/psum | solution.py:38
  1036.5 3.5 fusion.19
  1040.1 0.0 all-reduce.21.cloned.1.call-start
  1040.1 7.6 scatter_custom_fusion.6
  1047.7 63.4 %all-reduce.19.cloned.1.call-done = f32[16,2048]{1,0:T(8,128)} async-done(((f32[16,2048]{1,0:T(8,128)}), f32[16,2048]{1,0:T(8,128)}) %all-reduce.19.cloned.1.call-update) | async-done | bytes 131088 | tf_op jit(solution)/shard_map/psum | solution.py:45
  1111.1 1.0 multiply_reduce_fusion.2
  1112.1 11.7 psum.177
  1123.9 3.4 fusion.5
  1127.2 116.2 %psum.178 = bf16[1024,16]{0,1:T(8,128)(2,1)S(1)} all-reduce(bf16[1024,16]{0,1:T(8,128)(2,1)S(1)} %fusion.5), channel_id=1, replica_groups=mesh['sample'=4,'variant'=32,'trait'=4] {'variant'}, use_global_device_ids=true, to_apply=%region_30.31 | all-reduce | flops 16384 | bytes 65536 | tf_op jit(solution)/shard_map/psum | solution.py:38
  1243.4 3.5 fusion.20
  1246.9 0.0 all-reduce.23.cloned.1.call-start
  1247.0 7.6 scatter_custom_fusion.7
  1254.6 63.4 %all-reduce.21.cloned.1.call-done = f32[16,2048]{1,0:T(8,128)} async-done(((f32[16,2048]{1,0:T(8,128)}), f32[16,2048]{1,0:T(8,128)}) %all-reduce.21.cloned.1.call-update) | async-done | bytes 131088 | tf_op jit(solution)/shard_map/psum | solution.py:45
  1318.0 0.9 multiply_reduce_fusion.1
  1319.0 11.7 psum.180
  1330.7 3.4 fusion.6
  1334.1 116.2 %psum.181 = bf16[1024,16]{0,1:T(8,128)(2,1)S(1)} all-reduce(bf16[1024,16]{0,1:T(8,128)(2,1)S(1)} %fusion.6), channel_id=1, replica_groups=mesh['sample'=4,'variant'=32,'trait'=4] {'variant'}, use_global_device_ids=true, to_apply=%region_35.36 | all-reduce | flops 16384 | bytes 65536 | tf_op jit(solution)/shard_map/psum | solution.py:38
  1450.3 3.5 fusion.21
  1453.8 71.1 %all-reduce.23.cloned.1.call-done = f32[16,2048]{1,0:T(8,128)} async-done(((f32[16,2048]{1,0:T(8,128)}), f32[16,2048]{1,0:T(8,128)}) %all-reduce.23.cloned.1.call-update) | async-done | bytes 131088 | tf_op jit(solution)/shard_map/psum | solution.py:45
  1524.9 0.9 multiply_reduce_fusion
  1525.8 11.7 psum.183
  1537.6 1.6 broadcast_multiply_fusion
  (25 shorter events, 0.2 us)
Async XLA Ops:
  6.5 70.0 %all-reduce.9.cloned.1.call-start = ((), (), s32[]{:S(2)}) async-start(), calls=%async_computation | async-start | bytes 262144 | tf_op jit(solution)/shard_map/psum | solution.py:45
  15.3 193.6 %copy-start = (f32[1024,16]{0,1:T(8,128)S(1)}, f32[1024,16]{0,1:T(8,128)}, u32[]{:S(2)}) copy-start(f32[1024,16]{0,1:T(8,128)} %param.4) | copy-start | bytes 196612
  18.9 264.6 %all-reduce.11.cloned.1.call-start = ((), (), s32[]{:S(2)}) async-start(), calls=%async_computation.1 | async-start | bytes 262144 | tf_op jit(solution)/shard_map/psum | solution.py:45
  89.2 194.3 %copy-start.1 = (f32[16,2048]{1,0:T(8,128)S(1)}, f32[16,2048]{1,0:T(8,128)}, u32[]{:S(2)}) copy-start(f32[16,2048]{1,0:T(8,128)} %all-reduce.9.cloned.1.call-done) | copy-start | bytes 393220
  212.4 277.9 %all-reduce.13.cloned.1.call-start = ((), (), s32[]{:S(2)}) async-start(), calls=%async_computation.2 | async-start | bytes 262144 | tf_op jit(solution)/shard_map/psum | solution.py:45
  419.2 278.0 %all-reduce.15.cloned.1.call-start = ((), (), s32[]{:S(2)}) async-start(), calls=%async_computation.3 | async-start | bytes 262144 | tf_op jit(solution)/shard_map/psum | solution.py:45
  503.0 194.3 %copy-start.2 = (f32[16,2048]{1,0:T(8,128)S(1)}, f32[16,2048]{1,0:T(8,128)}, u32[]{:S(2)}) copy-start(f32[16,2048]{1,0:T(8,128)} %all-reduce.13.cloned.1.call-done) | copy-start | bytes 393220
  626.2 277.9 %all-reduce.17.cloned.1.call-start = ((), (), s32[]{:S(2)}) async-start(), calls=%async_computation.4 | async-start | bytes 262144 | tf_op jit(solution)/shard_map/psum | solution.py:45
  833.1 278.0 %all-reduce.19.cloned.1.call-start = ((), (), s32[]{:S(2)}) async-start(), calls=%async_computation.5 | async-start | bytes 262144 | tf_op jit(solution)/shard_map/psum | solution.py:45
  916.9 194.3 %copy-start.3 = (f32[16,2048]{1,0:T(8,128)S(1)}, f32[16,2048]{1,0:T(8,128)}, u32[]{:S(2)}) copy-start(f32[16,2048]{1,0:T(8,128)} %all-reduce.17.cloned.1.call-done) | copy-start | bytes 393220
  1040.1 277.9 %all-reduce.21.cloned.1.call-start = ((), (), s32[]{:S(2)}) async-start(), calls=%async_computation.6 | async-start | bytes 262144 | tf_op jit(solution)/shard_map/psum | solution.py:45
  1246.9 277.9 %all-reduce.23.cloned.1.call-start = ((), (), s32[]{:S(2)}) async-start(), calls=%async_computation.7 | async-start | bytes 262144 | tf_op jit(solution)/shard_map/psum | solution.py:45
Sparse Core Ops, SparseCore 0:
  19.0 57.4 all-reduce.8
  212.5 70.9 all-reduce.10
  419.4 70.9 all-reduce.12
  626.3 70.9 all-reduce.14
  833.2 70.9 all-reduce.16
  1040.2 70.9 all-reduce.18
  1247.1 70.9 all-reduce.20
  1453.9 70.9 all-reduce.22
where the time goes:
time: 1550 us
  blocking collectives  907 us (59%)
  waiting for transfers between devices  501 us (32%)
  other arithmetic  71.3 us (5%)
  matrix products  52 us (3%)
    psum x7, blocking collectives, on_device(): lax.psum(partial_sum.astype(jnp.bfloat16), 'variant').astype(jnp.float32)  813 us
    psum x8, waiting for transfers between devices, on_device(): gradient = lax.psum(grad_part, 'sample') * grad_scale  501 us
    psum x8, blocking collectives, trait_power(): return lax.psum(squares, 'trait')  93.8 us
    scatter-add x8, other arithmetic, on_device(): counts = jnp.zeros((local_rows,), jnp.float32).at[batch_rows[step]].add(1.0)  60.9 us
  transfers between devices with their start and end apart: 8, of which 8 were waited for; matrix products, arithmetic and copies ran while one was open for 3% of the time, Pallas kernels for 0%

commit v1 on v0

v1 whole, which is shorter than its diff:
```python
import functools
import math

import jax
import jax.numpy as jnp
from jax import lax
from jax.experimental import pallas as pl
from jax.experimental.pallas import tpu as pltpu
from jax.sharding import PartitionSpec as P

MESH = pl.DeviceIdType.MESH
LANES = 128
NT_DIMS = (((1,), (1,)), ((), ()))


def far_first(n):
    return sorted(range(n), key=lambda o: (-min(o, n - o), o))


def kernel(
    sizes, pred_scale, grad_scale,
    d_ref, ph_ref, rows_ref, out_ref,
    m_buf, gsend, gbuf, wsend, wbuf, psend, pbuf, dual, osend, obuf,
    g_ssem, g_rsem, w_ssem, w_rsem, p_ssem, p_rsem, m_ssem, m_rsem, o_ssem, o_rsem,
):
    ns, nv, nt, iters, nz = sizes
    nx = nv // nz
    chips = ns * nt // 2
    members = chips * 2
    s, v, t = lax.axis_index("sample"), lax.axis_index("variant"), lax.axis_index("trait")
    x, z = v // nz, lax.rem(v, nz)
    core = lax.rem(t, 2)
    y = (t // 2) * ns + s
    me = y * 2 + core

    def member_id(e):
        row = e // 2
        return (lax.rem(row, ns), v, (row // ns) * 2 + lax.rem(e, 2))

    def lanes(i):
        return pl.ds(pl.multiple_of(i * LANES, LANES), LANES)

    def remote(src, dst, ssem, rsem, device):
        return pltpu.make_async_remote_copy(
            src_ref=src, dst_ref=dst, send_sem=ssem, recv_sem=rsem, device_id=device, device_id_type=MESH
        )

    def wait_bytes(ref, sem):
        pltpu.make_async_copy(ref, ref, sem).wait()

    barrier = pltpu.get_barrier_semaphore()

    def greet_column(o, c):
        pl.semaphore_signal(
            barrier, inc=1, device_id=member_id(lax.rem(me + o, members)), device_id_type=MESH
        )
        return c

    def greet_plane(o, c):
        pl.semaphore_signal(barrier, inc=1, device_id=(s, lax.rem(v + o, nv), t), device_id_type=MESH)
        return c

    lax.fori_loop(1, members, greet_column, 0)
    lax.fori_loop(1, nv, greet_plane, 0)

    def counts_of(step, block):
        rows = rows_ref[pl.ds(step, 1), :]
        draws = rows.shape[1]
        ids = lax.broadcasted_iota(jnp.int32, (LANES, draws), 0) + block * LANES
        hot = jnp.where(rows == ids, 1.0, 0.0).astype(jnp.bfloat16)
        ones = jnp.ones((16, draws), jnp.bfloat16)
        return lax.dot_general(ones, hot, NT_DIMS, preferred_element_type=jnp.float32)

    for b in range(nz):
        cols = slice(b * LANES, (b + 1) * LANES)
        m_buf[:, cols] = (counts_of(0, b) * (0.0 - ph_ref[:, cols])).astype(jnp.bfloat16)
    dual[...] = jnp.zeros_like(dual)

    pl.semaphore_wait(barrier, members - 1 + nv - 1)

    def gradient(turn):
        misfit = m_buf[...]
        for o in far_first(chips):
            row = lax.rem(y + o, chips)
            cols = pl.ds(pl.multiple_of(row * 2 * LANES, 2 * LANES), 2 * LANES)
            part = jnp.dot(misfit, d_ref[:, cols], preferred_element_type=jnp.float32) * grad_scale
            for c in range(2):
                gsend[row * 2 + c] = part[:, c * LANES:(c + 1) * LANES]
            for c in range(2):
                e = row * 2 + c
                copy = remote(gsend.at[e], gbuf.at[me], g_ssem, g_rsem, member_id(e))
                if o:
                    copy.start()
                else:
                    pl.when(core != c)(copy.start)
        gbuf[me] = gsend[me]
        wait_bytes(gbuf.at[pl.ds(0, members - 1)], g_rsem)
        power = jnp.zeros((1, LANES), jnp.float32)
        turn_row = jnp.full((1, LANES), turn, jnp.float32)
        for g in range(nt):
            total = None
            for i in range(ns):
                share = gbuf[((g // 2) * ns + i) * 2 + g % 2]
                total = share if total is None else total + share
            old = dual[g]
            new = old + (total - old) / turn_row
            dual[g] = new
            power = power + jnp.sum(new * new, axis=0, keepdims=True)
        wait_bytes(gbuf.at[pl.ds(0, members - 1)], g_ssem)
        shrink = jnp.maximum(1.0 - 20.0 / jnp.sqrt(power + 1e-05), 0.0)
        return -jnp.sqrt(turn_row) * shrink

    def spread(src, dst, ssem, rsem):
        dst[:, lanes(me)] = src[t]

        def send(i, c):
            e = lax.rem(me + members // 2 + i, members)
            pl.when(e != me)(remote(src.at[member_id(e)[2]], dst.at[:, lanes(me)], ssem, rsem, member_id(e)).start)
            return c

        lax.fori_loop(0, members, send, 0)
        rest = dst.at[:, pl.ds(0, (members - 1) * LANES)]
        wait_bytes(rest, rsem)
        wait_bytes(rest, ssem)

    def iteration(turn, carry):
        factor = gradient(turn.astype(jnp.float32))
        for g in range(nt):
            wsend[g] = (factor * dual[g]).astype(jnp.bfloat16)
        spread(wsend, wbuf, w_ssem, w_rsem)

        side = lax.rem(turn, 2)
        weights = wbuf[...]
        pairs = nz // 2
        for o in far_first(pairs):
            pair = lax.rem(z // 2 + o, pairs)
            some = d_ref[pl.ds(pl.multiple_of(pair * 2 * LANES, 2 * LANES), 2 * LANES), :]
            part = lax.dot_general(weights, some, NT_DIMS, preferred_element_type=jnp.float32)
            for c in range(2):
                psend[pair * 2 + c] = part[:, c * LANES:(c + 1) * LANES].astype(jnp.bfloat16)
            for c in range(2):
                for ox in far_first(nx):
                    block = pair * 2 + c
                    to = lax.rem(x + ox, nx) * nz + block
                    copy = remote(psend.at[block], pbuf.at[side, v], p_ssem, p_rsem.at[side], (s, to, t))
                    if o or ox:
                        copy.start()
                    else:
                        pl.when(to != v)(copy.start)
        pbuf[side, v] = psend[z]
        counts = counts_of(turn, z)
        rest = pbuf.at[side, pl.ds(0, nv - 1)]
        wait_bytes(rest, p_rsem.at[side])
        total = jnp.sum(pbuf[side].astype(jnp.float32), axis=0)
        m_buf[:, lanes(z)] = (counts * (total * pred_scale - ph_ref[:, lanes(z)])).astype(jnp.bfloat16)

        def send(o, c):
            to = x * nz + lax.rem(z + o, nz)
            remote(m_buf.at[:, lanes(z)], m_buf.at[:, lanes(z)], m_ssem, m_rsem, (s, to, t)).start()
            return c

        lax.fori_loop(1, nz, send, 0)
        wait_bytes(rest, p_ssem)
        others = m_buf.at[:, pl.ds(0, (nz - 1) * LANES)]
        wait_bytes(others, m_rsem)
        wait_bytes(others, m_ssem)
        return carry

    lax.fori_loop(1, iters, iteration, 0)
    factor = gradient(jnp.float32(iters))
    for g in range(nt):
        osend[g] = factor * dual[g]
    spread(osend, obuf, o_ssem, o_rsem)
    out_ref[...] = obuf[...]


def on_device(sizes, pred_scale, grad_scale, dosages, phenotypes, batch_rows):
    ns, nv, nt, iters, nz = sizes
    samples, width = dosages.shape
    traits = phenotypes.shape[1]
    members = ns * nt
    f32, bf16 = jnp.float32, jnp.bfloat16
    vmem = pl.BlockSpec(memory_space=pltpu.VMEM)
    dma = pltpu.SemaphoreType.DMA
    return pl.pallas_call(
        functools.partial(kernel, sizes, pred_scale, grad_scale),
        out_shape=jax.ShapeDtypeStruct((traits, width), f32),
        in_specs=[vmem] * 3,
        out_specs=vmem,
        scratch_shapes=[
            pltpu.VMEM((traits, samples), bf16),
            pltpu.VMEM((members, traits, LANES), f32),
            pltpu.VMEM((members, traits, LANES), f32),
            pltpu.VMEM((nt, traits, LANES), bf16),
            pltpu.VMEM((traits, width), bf16),
            pltpu.VMEM((nz, traits, LANES), bf16),
            pltpu.VMEM((2, nv, traits, LANES), bf16),
            pltpu.VMEM((nt, traits, LANES), f32),
            pltpu.VMEM((nt, traits, LANES), f32),
            pltpu.VMEM((traits, width), f32),
            dma, dma, dma, dma, dma, dma((2,)), dma, dma, dma, dma,
        ],
        compiler_params=pltpu.CompilerParams(collective_id=0, has_side_effects=True),
        name="dual_averaging",
    )(dosages, phenotypes.T, batch_rows)


def solution(mesh):
    ns, nv, nt = mesh.shape["sample"], mesh.shape["variant"], mesh.shape["trait"]

    def whole(dosages, phenotypes, batch_rows):
        samples, variants = dosages.shape
        draws = batch_rows.shape[1]
        sizes = (ns, nv, nt, batch_rows.shape[0], samples // ns // LANES)
        return jax.shard_map(
            functools.partial(
                on_device, sizes, 0.06 * math.sqrt(draws) / variants, 1.0 / math.sqrt(draws)
            ),
            mesh=mesh,
            in_specs=(P("sample", "variant"), P("sample", "trait"), P(None, "sample")),
            out_specs=P("trait", "variant"),
            check_vma=False,
        )(dosages, phenotypes, batch_rows)

    return whole
```

time: 1550 us -> 189 us (0.12)
  blocking collectives: 907 us -> 0 us
  waiting for transfers between devices: 501 us -> 0 us
  Pallas kernels: 0 us -> 187 us
  other arithmetic: 71.3 us -> 0 us
  matrix products: 52 us -> 0 us
    psum x15 -> x0, blocking collectives: 907 us -> none  [the longest x7 813 us: on_device(): lax.psum(partial_sum.astype(jnp.bfloat16), 'variant').astype(jnp.float32)]
    psum x8 -> x0, waiting for transfers between devices: 501 us -> none  [on_device(): gradient = lax.psum(grad_part, 'sample') * grad_scale]
    pallas_call x0 -> x1, Pallas kernels: none -> 187 us  [on_device(): pl.pallas_call(functools.partial(kernel, sizes, pred_scale, grad_scale),...]
    scatter-add x8 -> x0, other arithmetic: 60.9 us -> none  [on_device(): counts = jnp.zeros((local_rows,), jnp.float32).at[batch_rows[step]].add(1.0)]
    dot_general x15 -> x0, matrix products: 52 us -> none  [the longest x8 28.1 us: on_device(): lax.dot_general(misfit, dosages, (((0,), (0,)), ((), ())), preferred_elem...]
  transfers between devices with their start and end apart: 8 -> 0, of which waited for: 8 -> 0; matrix products, arithmetic and copies ran while one was open for 3% -> 0% of each run, Pallas kernels for 0% -> 0%
where the time goes in v1:
time: 189 us
  Pallas kernels  187 us (99%)
    pallas_call x1, Pallas kernels, on_device(): pl.pallas_call(functools.partial(kernel, sizes, pred_scale, grad_scale),...  187 us

profile of v1, /device:TPU:1, one launch (start us, length us, event | category | flops | bytes accessed | tf_op | source)
XLA Modules:
  0.0 188.9 jit_solution(8118689591498922134)
XLA Ops:
  0.0 187.3 %dual_averaging.1 = f32[16,2048]{1,0:T(8,128)} custom-call(bf16[1024,2048]{1,0:T(8,128)(2,1)} %d_ref.1, f32[16,1024]{1,0:T(8,128)} %bitcast.1, s32[8,1024]{1,0:T(8,128)} %rows_ref.1), custom_call_target="tpu_custom_call" | custom-call | tf_op jit(solution)/shard_map/dual_averaging/pallas_call | solution.py:185
  187.4 1.6 copy.5

commit v2 on v1

v2 whole, which is shorter than its diff:
```python
import functools
import math

import jax
import jax.numpy as jnp
from jax import lax
from jax.experimental import pallas as pl
from jax.experimental.pallas import tpu as pltpu
from jax.sharding import PartitionSpec as P

MESH = pl.DeviceIdType.MESH
WIDE = 256
NT_DIMS = (((1,), (1,)), ((), ()))


def far_first(n):
    return sorted(range(n), key=lambda o: (-min(o, n - o), o))


def near(n):
    return range(-(n // 2), n - n // 2)


def kernel(
    sizes, pred_scale, grad_scale,
    d_hbm, ph_ref, rows_ref, out_ref,
    d_ref, m_buf, gsend, gbuf, wsend, wbuf, psend, pbuf, dual, osend, obuf,
    d_sem, g_ssem, g_rsem, w_ssem, w_rsem, p_ssem, p_rsem, m_ssem, m_rsem, o_ssem, o_rsem,
):
    ns, nv, nt, iters, blocks = sizes
    nz = blocks * 2
    nx = nv // nz
    reps = nt // 2
    chips = ns * reps
    members = chips * 2
    chunks = ns * 2
    half = m_buf.shape[1]
    samples = d_ref.shape[0]
    s, v, t = lax.axis_index("sample"), lax.axis_index("variant"), lax.axis_index("trait")
    x, z = v // nz, lax.rem(v, nz)
    core = lax.rem(t, 2)
    y = (t // 2) * ns + s
    me = y * 2 + core
    chunk = s * 2 + core
    upper, block = lax.rem(x, 2), lax.rem(z, blocks)

    def chip_device(row, c):
        return (lax.rem(row, ns), v, (row // ns) * 2 + c)

    def wide(i):
        return pl.ds(pl.multiple_of(i * WIDE, WIDE), WIDE)

    def remote(src, dst, ssem, rsem, device):
        return pltpu.make_async_remote_copy(
            src_ref=src, dst_ref=dst, send_sem=ssem, recv_sem=rsem, device_id=device, device_id_type=MESH
        )

    def wait_bytes(ref, sem):
        pltpu.make_async_copy(ref, ref, sem).wait()

    barrier = pltpu.get_barrier_semaphore()

    def greet_column(o, c):
        e = lax.rem(me + o, members)
        pl.semaphore_signal(
            barrier, inc=1, device_id=chip_device(e // 2, lax.rem(e, 2)), device_id_type=MESH
        )
        return c

    def greet_plane(o, c):
        pl.semaphore_signal(barrier, inc=1, device_id=(s, lax.rem(v + o, nv), t), device_id_type=MESH)
        return c

    lax.fori_loop(1, nv, greet_plane, 0)
    lax.fori_loop(1, members, greet_column, 0)
    for b in range(blocks):
        rows = pl.ds(b * WIDE, WIDE)
        pltpu.make_async_copy(d_hbm.at[rows], d_ref.at[rows], d_sem).start()

    def counts_of(step, b):
        rows = rows_ref[pl.ds(step, 1), :]
        draws = rows.shape[1]
        ids = lax.broadcasted_iota(jnp.int32, (WIDE, draws), 0) + b * WIDE
        hot = jnp.where(rows == ids, 1.0, 0.0).astype(jnp.bfloat16)
        ones = jnp.ones((2 * half, draws), jnp.bfloat16)
        return lax.dot_general(ones, hot, NT_DIMS, preferred_element_type=jnp.float32)

    for b in range(blocks):
        cols = slice(b * WIDE, (b + 1) * WIDE)
        first = counts_of(0, b) * (0.0 - ph_ref[:, cols])
        for h in range(2):
            m_buf[h, :, cols] = first[h * half:(h + 1) * half].astype(jnp.bfloat16)
    dual[...] = jnp.zeros_like(dual)
    wait_bytes(d_ref, d_sem)
    pl.semaphore_wait(barrier, members - 1 + nv - 1)

    def gradient(turn, side):
        misfit = jnp.concatenate([m_buf[0], m_buf[1]], axis=0)
        for o in far_first(ns)[::-1] if reps > 1 else far_first(ns):
            r = lax.rem(s + o, ns)
            for c in range(2):
                k = r * 2 + c
                part = jnp.dot(misfit, d_ref[:, wide(k)], preferred_element_type=jnp.float32)
                gsend[k] = (part * grad_scale).astype(jnp.bfloat16)
            for rep in range(reps)[::-1]:
                row = lax.rem((y // ns + rep) * ns, chips) + r
                for c in range(2):
                    copy = remote(
                        gsend.at[r * 2 + c], gbuf.at[side, me], g_ssem, g_rsem.at[side], chip_device(row, c)
                    )
                    if o or rep:
                        copy.start()
                    else:
                        pl.when(core != c)(copy.start)
        gbuf[side, me] = gsend[chunk]
        rest = gbuf.at[side, pl.ds(0, members - 1)]
        wait_bytes(rest, g_rsem.at[side])
        power = jnp.zeros((1, WIDE), jnp.float32)
        turn_row = jnp.full((1, WIDE), turn, jnp.float32)
        for g in range(nt):
            total = None
            for i in range(ns):
                share = gbuf[side, ((g // 2) * ns + i) * 2 + g % 2].astype(jnp.float32)
                total = share if total is None else total + share
            old = dual[g]
            fresh = old + (total - old) / turn_row
            dual[g] = fresh
            power = power + jnp.sum(fresh * fresh, axis=0, keepdims=True)
        shrink = jnp.maximum(1.0 - 20.0 / jnp.sqrt(power + 1e-05), 0.0)
        return jnp.sqrt(turn_row) * shrink, rest

    def spread(src, dst, ssem, rsem):
        for o in sorted(near(ns), key=lambda o: -abs(o)):
            row = lax.rem(y + o + chips, chips)
            for c in range(2):
                g = (row // ns) * 2 + c
                copy = remote(src.at[g], dst.at[:, wide(chunk)], ssem, rsem, chip_device(row, c))
                if o:
                    copy.start()
                else:
                    pl.when(core != c)(copy.start)
        dst[:, wide(chunk)] = src[t]
        return dst.at[:, pl.ds(0, (chunks - 1) * WIDE)]

    def iteration(turn, carry):
        side = lax.rem(turn, 2)
        factor, sent = gradient(turn.astype(jnp.float32), side)
        for g in range(nt):
            wsend[g] = (0.0 - factor * dual[g]).astype(jnp.bfloat16)
        rest = spread(wsend, wbuf, w_ssem, w_rsem)
        wait_bytes(sent, g_ssem)
        counts = counts_of(turn, block)[:half]
        wait_bytes(rest, w_rsem)
        wait_bytes(rest, w_ssem)

        weights = wbuf[...]
        for o in far_first(blocks)[::-1]:
            b = lax.rem(block + o, blocks)
            part = lax.dot_general(weights, d_ref[wide(b), :], NT_DIMS, preferred_element_type=jnp.float32)
            for h in range(2):
                psend[b, h] = part[h * half:(h + 1) * half].astype(jnp.bfloat16)
            for oz in sorted((o, o + blocks), key=lambda a: -min(a, nz - a)):
                for ox in far_first(nx):
                    tx = lax.rem(x + ox, nx)
                    to = tx * nz + lax.rem(z + oz, nz)
                    copy = remote(
                        psend.at[b, lax.rem(tx, 2)], pbuf.at[side, v], p_ssem, p_rsem.at[side], (s, to, t)
                    )
                    if ox or oz:
                        copy.start()
        pbuf[side, v] = psend[block, upper]
        rest = pbuf.at[side, pl.ds(0, nv - 1)]
        wait_bytes(rest, p_rsem.at[side])
        total = jnp.sum(pbuf[side].astype(jnp.float32), axis=0)
        traits = pl.ds(pl.multiple_of(upper * half, half), half)
        m_buf[upper, :, wide(block)] = (
            counts * (total * pred_scale - ph_ref[traits, wide(block)])
        ).astype(jnp.bfloat16)
        own = m_buf.at[upper, :, wide(block)]
        for other in (1, 0):
            tx = x + other * (1 - 2 * upper)
            for oz in sorted(near(blocks), key=lambda o: -abs(o)):
                if other or oz:
                    to = tx * nz + lax.rem(z + oz + nz, nz)
                    remote(own, own, m_ssem, m_rsem, (s, to, t)).start()
        wait_bytes(rest, p_ssem)
        for sem in (m_rsem, m_ssem):
            wait_bytes(pbuf.at[1 - side, pl.ds(0, 2 * blocks - 1)], sem)
        return carry

    lax.fori_loop(1, iters, iteration, 0)
    factor, sent = gradient(jnp.float32(iters), iters % 2)
    for g in range(nt):
        osend[g] = factor * dual[g]
    rest = spread(osend, obuf, o_ssem, o_rsem)
    wait_bytes(sent, g_ssem)
    wait_bytes(rest, o_rsem)
    wait_bytes(rest, o_ssem)
    out_ref[...] = obuf[...]


def on_device(sizes, pred_scale, grad_scale, dosages, phenotypes, batch_rows):
    ns, nv, nt, iters, blocks = sizes
    samples, width = dosages.shape
    traits = phenotypes.shape[1]
    members = ns * nt
    half = traits // 2
    f32, bf16 = jnp.float32, jnp.bfloat16
    vmem = pl.BlockSpec(memory_space=pltpu.VMEM)
    dma = pltpu.SemaphoreType.DMA
    negated = pl.pallas_call(
        functools.partial(kernel, sizes, pred_scale, grad_scale),
        out_shape=jax.ShapeDtypeStruct((traits, width), f32),
        in_specs=[pl.BlockSpec(memory_space=pl.ANY), vmem, vmem],
        out_specs=vmem,
        scratch_shapes=[
            pltpu.VMEM((samples, width), bf16),
            pltpu.VMEM((2, half, samples), bf16),
            pltpu.VMEM((ns * 2, traits, WIDE), bf16),
            pltpu.VMEM((2, members, traits, WIDE), bf16),
            pltpu.VMEM((nt, traits, WIDE), bf16),
            pltpu.VMEM((traits, width), bf16),
            pltpu.VMEM((blocks, 2, half, WIDE), bf16),
            pltpu.VMEM((2, nv, half, WIDE), bf16),
            pltpu.VMEM((nt, traits, WIDE), f32),
            pltpu.VMEM((nt, traits, WIDE), f32),
            pltpu.VMEM((traits, width), f32),
            dma, dma, dma((2,)), dma, dma, dma, dma((2,)), dma, dma, dma, dma,
        ],
        compiler_params=pltpu.CompilerParams(collective_id=0, has_side_effects=True),
        name="dual_averaging",
    )(dosages, phenotypes.T, batch_rows)
    return -negated


def solution(mesh):
    ns, nv, nt = mesh.shape["sample"], mesh.shape["variant"], mesh.shape["trait"]

    def whole(dosages, phenotypes, batch_rows):
        samples, variants = dosages.shape
        draws = batch_rows.shape[1]
        sizes = (ns, nv, nt, batch_rows.shape[0], samples // ns // WIDE)
        return jax.shard_map(
            functools.partial(
                on_device, sizes, 0.06 * math.sqrt(draws) / variants, 1.0 / math.sqrt(draws)
            ),
            mesh=mesh,
            in_specs=(P("sample", "variant"), P("sample", "trait"), P(None, "sample")),
            out_specs=P("trait", "variant"),
            check_vma=False,
        )(dosages, phenotypes, batch_rows)

    return whole
```

time: 189 us -> 176 us (0.931)
  Pallas kernels: 187 us -> 174 us
    pallas_call x1, Pallas kernels: 187 us -> 174 us  [on_device(): pl.pallas_call(functools.partial(kernel, sizes, pred_scale, grad_scale),...]
where the time goes in v2:
time: 176 us; the launch traced here: 175 us
  Pallas kernels  174 us (99%)
    pallas_call x1, Pallas kernels, on_device(): pl.pallas_call(functools.partial(kernel, sizes, pred_scale, grad_scale),...  174 us

profile of v2, /device:TPU:1, one launch (start us, length us, event | category | flops | bytes accessed | tf_op | source)
XLA Modules:
  0.0 175.4 jit_solution(13359885609162405580)
XLA Ops:
  0.0 173.9 %dual_averaging.1 = f32[16,2048]{1,0:T(8,128)} custom-call(bf16[1024,2048]{1,0:T(8,128)(2,1)} %d_hbm.1, f32[16,1024]{1,0:T(8,128)} %bitcast.1, s32[8,1024]{1,0:T(8,128)} %rows_ref.1), custom_call_target="tpu_custom_call" | custom-call | tf_op jit(solution)/shard_map/dual_averaging/pallas_call | solution.py:211
  173.9 1.6 neg.3

commit v3 on v2

--- a/solution.py
+++ b/solution.py
@@ -17,8 +17,11 @@
     return sorted(range(n), key=lambda o: (-min(o, n - o), o))
 
 
-def near(n):
-    return range(-(n // 2), n - n // 2)
+def near(n, place):
+    if n == 1:
+        return [0]
+    inner = sorted(range(1 - n // 2, n // 2), key=lambda o: -abs(o))
+    return [n // 2 * (1 - 2 * (place // (n // 2)))] + inner
 
 
 def kernel(
@@ -130,12 +133,12 @@
         return jnp.sqrt(turn_row) * shrink, rest
 
     def spread(src, dst, ssem, rsem):
-        for o in sorted(near(ns), key=lambda o: -abs(o)):
+        for i, o in enumerate(near(ns, s)):
             row = lax.rem(y + o + chips, chips)
             for c in range(2):
                 g = (row // ns) * 2 + c
                 copy = remote(src.at[g], dst.at[:, wide(chunk)], ssem, rsem, chip_device(row, c))
-                if o:
+                if i < ns - 1:
                     copy.start()
                 else:
                     pl.when(core != c)(copy.start)
@@ -179,8 +182,8 @@
         own = m_buf.at[upper, :, wide(block)]
         for other in (1, 0):
             tx = x + other * (1 - 2 * upper)
-            for oz in sorted(near(blocks), key=lambda o: -abs(o)):
-                if other or oz:
+            for i, oz in enumerate(near(blocks, block)):
+                if other or i < blocks - 1:
                     to = tx * nz + lax.rem(z + oz + nz, nz)
                     remote(own, own, m_ssem, m_rsem, (s, to, t)).start()
         wait_bytes(rest, p_ssem)

time: 176 us -> 172 us (0.977)
  Pallas kernels: 174 us -> 170 us
    pallas_call x1, Pallas kernels: 174 us -> 170 us  [on_device(): pl.pallas_call(functools.partial(kernel, sizes, pred_scale, grad_scale),...]
where the time goes in v3:
time: 172 us
  Pallas kernels  170 us (99%)
    pallas_call x1, Pallas kernels, on_device(): pl.pallas_call(functools.partial(kernel, sizes, pred_scale, grad_scale),...  170 us

profile of v3, /device:TPU:1, one launch (start us, length us, event | category | flops | bytes accessed | tf_op | source)
XLA Modules:
  0.0 171.7 jit_solution(8187354299287621018)
XLA Ops:
  0.0 170.1 %dual_averaging.1 = f32[16,2048]{1,0:T(8,128)} custom-call(bf16[1024,2048]{1,0:T(8,128)(2,1)} %d_hbm.1, f32[16,1024]{1,0:T(8,128)} %bitcast.1, s32[8,1024]{1,0:T(8,128)} %rows_ref.1), custom_call_target="tpu_custom_call" | custom-call | tf_op jit(solution)/shard_map/dual_averaging/pallas_call | solution.py:214
  170.1 1.6 neg.3

commit v4 on v3

--- a/solution.py
+++ b/solution.py
@@ -130,7 +130,7 @@
             dual[g] = fresh
             power = power + jnp.sum(fresh * fresh, axis=0, keepdims=True)
         shrink = jnp.maximum(1.0 - 20.0 / jnp.sqrt(power + 1e-05), 0.0)
-        return jnp.sqrt(turn_row) * shrink, rest
+        return jnp.sqrt(turn_row) * shrink
 
     def spread(src, dst, ssem, rsem):
         for i, o in enumerate(near(ns, s)):
@@ -145,16 +145,17 @@
         dst[:, wide(chunk)] = src[t]
         return dst.at[:, pl.ds(0, (chunks - 1) * WIDE)]
 
-    def iteration(turn, carry):
+    g_sent = gbuf.at[0, pl.ds(0, members - 1)]
+    p_sent = pbuf.at[0, pl.ds(0, nv - 1)]
+    m_sent = pbuf.at[0, pl.ds(0, 2 * blocks - 1)]
+
+    def iteration(turn, factor):
         side = lax.rem(turn, 2)
-        factor, sent = gradient(turn.astype(jnp.float32), side)
         for g in range(nt):
             wsend[g] = (0.0 - factor * dual[g]).astype(jnp.bfloat16)
-        rest = spread(wsend, wbuf, w_ssem, w_rsem)
-        wait_bytes(sent, g_ssem)
+        w_sent = spread(wsend, wbuf, w_ssem, w_rsem)
         counts = counts_of(turn, block)[:half]
-        wait_bytes(rest, w_rsem)
-        wait_bytes(rest, w_ssem)
+        wait_bytes(w_sent, w_rsem)
 
         weights = wbuf[...]
         for o in far_first(blocks)[::-1]:
@@ -186,17 +187,19 @@
                 if other or i < blocks - 1:
                     to = tx * nz + lax.rem(z + oz + nz, nz)
                     remote(own, own, m_ssem, m_rsem, (s, to, t)).start()
-        wait_bytes(rest, p_ssem)
-        for sem in (m_rsem, m_ssem):
-            wait_bytes(pbuf.at[1 - side, pl.ds(0, 2 * blocks - 1)], sem)
-        return carry
-
-    lax.fori_loop(1, iters, iteration, 0)
-    factor, sent = gradient(jnp.float32(iters), iters % 2)
+        wait_bytes(g_sent, g_ssem)
+        wait_bytes(w_sent, w_ssem)
+        wait_bytes(m_sent, m_rsem)
+        factor = gradient((turn + 1).astype(jnp.float32), 1 - side)
+        wait_bytes(p_sent, p_ssem)
+        wait_bytes(m_sent, m_ssem)
+        return factor
+
+    factor = lax.fori_loop(1, iters, iteration, gradient(jnp.float32(1), 1))
     for g in range(nt):
         osend[g] = factor * dual[g]
     rest = spread(osend, obuf, o_ssem, o_rsem)
-    wait_bytes(sent, g_ssem)
+    wait_bytes(g_sent, g_ssem)
     wait_bytes(rest, o_rsem)
     wait_bytes(rest, o_ssem)
     out_ref[...] = obuf[...]

time: 172 us -> 173 us (level)
  no operation moved by 1% of the time
where the time goes in v4:
time: 173 us; the launch traced here: 172 us
  Pallas kernels  171 us (99%)
    pallas_call x1, Pallas kernels, on_device(): pl.pallas_call(functools.partial(kernel, sizes, pred_scale, grad_scale),...  171 us

profile of v4, /device:TPU:1, one launch (start us, length us, event | category | flops | bytes accessed | tf_op | source)
XLA Modules:
  0.0 172.4 jit_solution(15446480583192024670)
XLA Ops:
  0.0 170.8 %dual_averaging.1 = f32[16,2048]{1,0:T(8,128)} custom-call(bf16[1024,2048]{1,0:T(8,128)(2,1)} %d_hbm.1, f32[16,1024]{1,0:T(8,128)} %bitcast.1, s32[8,1024]{1,0:T(8,128)} %rows_ref.1), custom_call_target="tpu_custom_call" | custom-call | tf_op jit(solution)/shard_map/dual_averaging/pallas_call | solution.py:217
  170.8 1.6 neg.3

commit v5 on v3

--- a/solution.py
+++ b/solution.py
@@ -63,15 +63,18 @@
 
     barrier = pltpu.get_barrier_semaphore()
 
+    def far(o, n):
+        return lax.rem(o - 1 + n // 2, n - 1) + 1
+
     def greet_column(o, c):
-        e = lax.rem(me + o, members)
+        e = lax.rem(me + far(o, members), members)
         pl.semaphore_signal(
             barrier, inc=1, device_id=chip_device(e // 2, lax.rem(e, 2)), device_id_type=MESH
         )
         return c
 
     def greet_plane(o, c):
-        pl.semaphore_signal(barrier, inc=1, device_id=(s, lax.rem(v + o, nv), t), device_id_type=MESH)
+        pl.semaphore_signal(barrier, inc=1, device_id=(s, lax.rem(v + far(o, nv), nv), t), device_id_type=MESH)
         return c
 
     lax.fori_loop(1, nv, greet_plane, 0)
@@ -105,11 +108,10 @@
                 k = r * 2 + c
                 part = jnp.dot(misfit, d_ref[:, wide(k)], preferred_element_type=jnp.float32)
                 gsend[k] = (part * grad_scale).astype(jnp.bfloat16)
-            for rep in range(reps)[::-1]:
-                row = lax.rem((y // ns + rep) * ns, chips) + r
-                for c in range(2):
+                for rep in range(reps)[::-1]:
+                    row = lax.rem((y // ns + rep) * ns, chips) + r
                     copy = remote(
-                        gsend.at[r * 2 + c], gbuf.at[side, me], g_ssem, g_rsem.at[side], chip_device(row, c)
+                        gsend.at[k], gbuf.at[side, me], g_ssem, g_rsem.at[side], chip_device(row, c)
                     )
                     if o or rep:
                         copy.start()

time: 172 us -> 176 us (1.023)
  Pallas kernels: 170 us -> 175 us
    pallas_call x1, Pallas kernels: 170 us -> 175 us  [on_device(): pl.pallas_call(functools.partial(kernel, sizes, pred_scale, grad_scale),...]
where the time goes in v5:
time: 176 us
  Pallas kernels  175 us (99%)
    pallas_call x1, Pallas kernels, on_device(): pl.pallas_call(functools.partial(kernel, sizes, pred_scale, grad_scale),...  175 us

profile of v5, /device:TPU:1, one launch (start us, length us, event | category | flops | bytes accessed | tf_op | source)
XLA Modules:
  0.0 176.1 jit_solution(16304263773426194587)
XLA Ops:
  0.0 174.5 %dual_averaging.1 = f32[16,2048]{1,0:T(8,128)} custom-call(bf16[1024,2048]{1,0:T(8,128)(2,1)} %d_hbm.1, f32[16,1024]{1,0:T(8,128)} %bitcast.1, s32[8,1024]{1,0:T(8,128)} %rows_ref.1), custom_call_target="tpu_custom_call" | custom-call | tf_op jit(solution)/shard_map/dual_averaging/pallas_call | solution.py:216
  174.5 1.6 neg.3
